TPU v7x, 256 devices: a whole 4x4x8 slice. The times are simulated.
256 devices in a mesh: seq: 32 (over z, y), tp: 8 (over x, core).
Axes of the slice: x: 4, y: 4, z: 8, core: 2. Of those that a mesh axis runs over, the one named last changes fastest.
Arguments:
- query_raw: bfloat16 [16384, 4096], P('seq', 'tp'), may hold values from -6 to 6
- key_raw: bfloat16 [16384, 4096], P('seq', 'tp'), may hold values from -6 to 6
- value_raw: bfloat16 [16384, 4096], P('seq', 'tp'), may hold values from -6 to 6
- conv_taps: float32 [3, 4, 4096], P(None, None, 'tp'), may hold values from -3 to 3
- layout_boxes: int32 [4, 16384], P(None, 'seq'), may hold values from 0 to 1023
- box_tables: bfloat16 [2, 1024, 4096], P(None, None, 'tp'), may hold values from -4 to 4
- log_decay: float32 [32, 16384], P('tp', 'seq'), may hold values from -1 to 0, as said below
- norm_gain: float32 [4096], P('tp'), may hold values from 0.25 to 1.75
- out_weight: bfloat16 [4096, 4096], P('tp', 'seq'), may hold values from -0.09375 to 0.09375
- grad_output: bfloat16 [16384, 4096], P('seq', 'tp'), may hold values from -6 to 6
Outputs:
- layer_out: bfloat16 [16384, 4096], P('seq', 'tp')
- grad_query: bfloat16 [16384, 4096], P('seq', 'tp')
- grad_key: bfloat16 [16384, 4096], P('seq', 'tp')
- grad_value: bfloat16 [16384, 4096], P('seq', 'tp')
- grad_taps: float32 [3, 4, 4096], P(None, None, 'tp')
- grad_tables: float32 [2, 1024, 4096], P(None, None, 'tp')
- grad_gain: float32 [4096], P('tp')
- grad_weight: float32 [4096, 4096], P('tp', 'seq')
Inputs may be any that keep to these rules, and one draw needn't show every extreme that they name: `log_decay`: each entry is the logarithm (at most 0) of one head's state decay at one token.
All inputs are finite; a program needn't handle non-finite values.
Results may differ from a plain program's by a relative error of at most 0.02.
Values may be sent and summed in bfloat16 or wider, within the bound.
A program may use at most 128 MiB of HBM per device.

v0:
```python
import jax
import jax.numpy as jnp
from jax import lax
from jax.sharding import PartitionSpec as P

HIGHEST = lax.Precision.HIGHEST


def shifted(x, axis, by):
    length = lax.axis_size(axis)
    pairs = [(i, i + by) for i in range(length) if 0 <= i + by < length]
    return lax.ppermute(x, axis, pairs)


def entering(x, axis, combine, identity, reverse):
    length, here = (lax.axis_size(axis), lax.axis_index(axis))
    everything = jax.tree.map(
        lambda part, kind: lax.all_gather(part.astype(kind), axis), x, (jnp.bfloat16, jnp.bfloat16)
    )
    start = jax.tree.map(
        lambda part, zero: jnp.broadcast_to(jnp.asarray(zero, part.dtype), part.shape), x, identity
    )

    def turn(k, before):
        at = length - 1 - k if reverse else k
        reached = at > here if reverse else at < here
        new = combine(
            before, jax.tree.map(lambda part, own: part[at].astype(own.dtype), everything, x)
        )
        return jax.tree.map(lambda a, b: jnp.where(reached, a, b), new, before)

    return lax.fori_loop(0, length, turn, start)


def combine(earlier, later):
    return (earlier[0] * later[0], later[0][:, None, None] * earlier[1] + later[1])


def on_device(
    query_raw,
    key_raw,
    value_raw,
    conv_taps,
    layout_boxes,
    box_tables,
    log_decay,
    norm_gain,
    out_weight,
    grad_output,
):
    row_count, feat_width = query_raw.shape
    head_count = log_decay.shape[0]
    head_size = feat_width // head_count
    kernel = conv_taps.shape[1]
    buckets = box_tables.shape[1]
    feature_scale = head_size ** (-0.5)
    stacked = jnp.stack([query_raw, key_raw, value_raw])
    rim_rows = shifted(stacked[:, row_count - (kernel - 1) :, :], "seq", 1)
    padded = jnp.concatenate([rim_rows, stacked], axis=1).astype(jnp.float32)
    conved = jnp.zeros((3, row_count, feat_width), jnp.float32)
    for tap_step in range(kernel):
        conved = (
            conved
            + conv_taps[:, tap_step, None, :]
            * padded[:, kernel - 1 - tap_step : kernel - 1 - tap_step + row_count, :]
        )
    bucket_ids = jnp.arange(buckets, dtype=jnp.int32)

    def count_table(first, second):
        return (first[:, None] == bucket_ids[None, :]).astype(jnp.bfloat16) + (
            second[:, None] == bucket_ids[None, :]
        ).astype(jnp.bfloat16)

    hot_x = count_table(layout_boxes[0], layout_boxes[2])
    hot_y = count_table(layout_boxes[1], layout_boxes[3])
    layout = jnp.dot(hot_x, box_tables[0], preferred_element_type=jnp.float32) + jnp.dot(
        hot_y, box_tables[1], preferred_element_type=jnp.float32
    )
    query_feat = (feature_scale * (conved[0] + layout)).astype(jnp.bfloat16)
    key_feat = (conved[1] + layout).astype(jnp.bfloat16)
    value_feat = conved[2].astype(jnp.bfloat16)

    def split_heads(matrix):
        return matrix.reshape(row_count, head_count, head_size).transpose(1, 0, 2)

    def join_heads(blocks):
        return blocks.transpose(1, 0, 2).reshape(row_count, feat_width)

    query_heads = split_heads(query_feat)
    key_heads = split_heads(key_feat)
    value_heads = split_heads(value_feat)
    decay_sum = jnp.cumsum(log_decay, axis=1)
    decay_total = decay_sum[:, -1]
    head_decay = jnp.exp(decay_sum)[:, :, None]
    tail_decay = jnp.exp(decay_total[:, None] - decay_sum)[:, :, None]
    block_decay = jnp.exp(decay_total)
    positions = jnp.arange(row_count, dtype=jnp.int32)
    causal_mask = positions[:, None] >= positions[None, :]
    decay_mask = jnp.where(
        causal_mask[None],
        jnp.exp(jnp.minimum(decay_sum[:, :, None] - decay_sum[:, None, :], 0.0)),
        0.0,
    )
    identity = (
        jnp.ones((head_count,), jnp.float32),
        jnp.zeros((head_count, head_size, head_size), jnp.float32),
    )
    local_state = jnp.einsum("hsi,hsj->hij", key_heads * tail_decay, value_heads, precision=HIGHEST)
    incoming = entering((block_decay, local_state), "seq", combine, identity, False)[1]
    scores = decay_mask * jnp.einsum(
        "hti,hsi->hts", query_heads, key_heads, preferred_element_type=jnp.float32
    )
    attended = jnp.einsum("hts,hsj->htj", scores, value_heads, precision=HIGHEST)
    attended = attended + head_decay * jnp.einsum(
        "hti,hij->htj", query_heads, incoming, precision=HIGHEST
    )
    inverse = lax.rsqrt(jnp.mean(attended * attended, axis=-1, keepdims=True) + 1e-06)
    unit_norm = attended * inverse
    gain_heads = norm_gain.reshape(head_count, 1, head_size)
    normed = join_heads(unit_norm * gain_heads).astype(jnp.bfloat16)
    partial_sum = jnp.dot(
        normed,
        lax.all_gather(out_weight, "seq", axis=1, tiled=True),
        preferred_element_type=jnp.float32,
    )
    layer_out = lax.psum_scatter(
        partial_sum.astype(jnp.bfloat16), "tp", scatter_dimension=1, tiled=True
    )
    cotangent = lax.all_gather(grad_output, "tp", axis=1, tiled=True)
    contract_last = (((1,), (1,)), ((), ()))
    grad_normed_sum = lax.dot_general(
        cotangent,
        lax.all_gather(out_weight, "seq", axis=1, tiled=True),
        contract_last,
        preferred_element_type=jnp.float32,
    )
    grad_normed = grad_normed_sum.astype(jnp.bfloat16)
    contract_first = (((0,), (0,)), ((), ()))
    weight_terms = lax.dot_general(
        normed, cotangent, contract_first, preferred_element_type=jnp.float32
    )
    grad_weight = lax.psum_scatter(
        weight_terms.astype(jnp.bfloat16), "seq", scatter_dimension=1, tiled=True
    ).astype(jnp.float32)
    grad_heads = split_heads(grad_normed).astype(jnp.float32)
    gain_terms = jnp.sum(grad_heads * unit_norm, axis=1).reshape(feat_width)
    grad_unit = grad_heads * gain_heads
    grad_attended = inverse * (
        grad_unit - unit_norm * jnp.mean(grad_unit * unit_norm, axis=-1, keepdims=True)
    )
    back_state = jnp.einsum(
        "hti,htj->hij", query_heads * head_decay, grad_attended, precision=HIGHEST
    )
    later_state = entering((block_decay, back_state), "seq", combine, identity, True)[1]
    grad_scores = decay_mask * jnp.einsum(
        "htj,hsj->hts", grad_attended, value_heads, precision=HIGHEST
    )
    grad_qh = jnp.einsum(
        "hts,hsi->hti", grad_scores, key_heads, precision=HIGHEST
    ) + head_decay * jnp.einsum("htj,hij->hti", grad_attended, incoming, precision=HIGHEST)
    grad_kh = jnp.einsum(
        "hts,hti->hsi", grad_scores, query_heads, precision=HIGHEST
    ) + tail_decay * jnp.einsum("hsj,hij->hsi", value_heads, later_state, precision=HIGHEST)
    grad_vh = jnp.einsum(
        "hts,htj->hsj", scores, grad_attended, precision=HIGHEST
    ) + tail_decay * jnp.einsum("hsi,hij->hsj", key_heads, later_state, precision=HIGHEST)
    grad_pre = jnp.stack(
        [feature_scale * join_heads(grad_qh), join_heads(grad_kh), join_heads(grad_vh)]
    )
    next_rows = shifted(grad_pre[:, : kernel - 1, :], "seq", -1)
    extended = jnp.concatenate([grad_pre, next_rows], axis=1)
    grad_inputs = jnp.zeros((3, row_count, feat_width), jnp.float32)
    for tap_step in range(kernel):
        grad_inputs = (
            grad_inputs
            + conv_taps[:, tap_step, None, :] * extended[:, tap_step : tap_step + row_count, :]
        )
    tap_terms = jnp.stack(
        [
            jnp.sum(
                grad_pre * padded[:, kernel - 1 - tap_step : kernel - 1 - tap_step + row_count, :],
                axis=1,
            )
            for tap_step in range(kernel)
        ],
        axis=1,
    )
    grad_layout = (grad_pre[0] + grad_pre[1]).astype(jnp.bfloat16)
    table_terms = jnp.stack(
        [
            lax.dot_general(hot_x, grad_layout, contract_first, preferred_element_type=jnp.float32),
            lax.dot_general(hot_y, grad_layout, contract_first, preferred_element_type=jnp.float32),
        ]
    )
    grad_taps, grad_tables, grad_gain = (
        lax.psum(tap_terms.astype(jnp.bfloat16), "seq").astype(jnp.float32),
        lax.psum(table_terms.astype(jnp.bfloat16), "seq").astype(jnp.float32),
        lax.psum(gain_terms.astype(jnp.bfloat16), "seq").astype(jnp.float32),
    )
    grad_query = grad_inputs[0].astype(jnp.bfloat16)
    grad_key = grad_inputs[1].astype(jnp.bfloat16)
    grad_value = grad_inputs[2].astype(jnp.bfloat16)
    return (
        layer_out,
        grad_query,
        grad_key,
        grad_value,
        grad_taps,
        grad_tables,
        grad_gain,
        grad_weight,
    )


def solution(mesh):
    return jax.shard_map(
        on_device,
        mesh=mesh,
        in_specs=(
            P("seq", "tp"),
            P("seq", "tp"),
            P("seq", "tp"),
            P(None, None, "tp"),
            P(None, "seq"),
            P(None, None, "tp"),
            P("tp", "seq"),
            P("tp"),
            P("tp", "seq"),
            P("seq", "tp"),
        ),
        out_specs=(
            P("seq", "tp"),
            P("seq", "tp"),
            P("seq", "tp"),
            P("seq", "tp"),
            P(None, None, "tp"),
            P(None, None, "tp"),
            P("tp"),
            P("tp", "seq"),
        ),
        check_vma=False,
    )
```

profile of v0, /device:TPU:8, one launch (start us, length us, event | category | flops | bytes accessed | tf_op | source)
XLA Modules:
  0.0 769.7 jit_solution(2590251355340707665)
XLA Ops:
  12.7 3.5 collective-permute-start
  20.4 5.0 collective-permute-done
  26.3 3.7 multiply_add_fusion
  35.2 74.4 %all-reduce = bf16[128]{0:T(256)(128)(2,1)S(1)} all-reduce(bf16[128]{0:T(256)(128)(2,1)S(1)} %dynamic-update-slice), channel_id=2, replica_groups=mesh['seq'=32,'tp'=8] {'seq'}, use_global_device_ids=true, to_apply=%add | all-reduce | flops 128 | bytes 512
  112.6 20.2 %all-gather.8.cloned.1.call-done = bf16[512,4096]{1,0:T(8,128)(2,1)} async-done(((bf16[512,128]{1,0:T(8,128)(2,1)}), bf16[512,4096]{1,0:T(8,128)(2,1)}) %all-gather.8.cloned.1.call-update) | async-done | bytes 4194320 | tf_op jit(solution)/shard_map/all_gather | solution.py:123
  132.8 5.8 convolution_convert_fusion.4
  138.7 78.2 %all-gather.12.cloned.1.call-done = bf16[128,128,128]{2,1,0:T(8,128)(2,1)} async-done(((bf16[4,128,128]{2,1,0:T(8,128)(2,1)}), bf16[128,128,128]{2,1,0:T(8,128)(2,1)}) %all-gather.12.cloned.1.call-update) | async-done | bytes 4194320 | tf_op jit(solution)/shard_map/all_gather | solution.py:18
  216.9 33.9 %while.30 = (s32[]{:T(128)}, f32[4,128,128]{2,1,0:T(8,128)S(1)}, s32[]{:T(128)}, bf16[32,4]{1,0:T(8,128)(2,1)S(1)}, bf16[32,4,128,128]{3,2,1,0:T(8,128)(2,1)}, /*index=5*/s32[]{:T(128)}, s32[]{:T(128)}) while((s32[]{:T(128)}, f32[4,128,128]{2,1,0:T(8,128)S(1)}, s32[]{:T(128)}, bf16[32,4]{1,0:T(8,128)(2,1)S(1)}, ...), condition=%wide.region_3.4_spmd.clone, body=%wide.region_2.3_spmd.clone.sunk | while | flops 327688 | bytes 655513 | solution.py:32
  252.4 6.7 multiply_reduce_fusion.4
  264.5 6.5 convolution_convert_fusion
  271.0 6.5 copy.96
  279.5 3.9 fusion.39
  283.3 4.5 fusion.36
  287.9 52.6 %all-gather.14.cloned.1.call-done = bf16[128,128,128]{2,1,0:T(8,128)(2,1)} async-done(((bf16[4,128,128]{2,1,0:T(8,128)(2,1)}), bf16[128,128,128]{2,1,0:T(8,128)(2,1)}) %all-gather.14.cloned.1.call-update) | async-done | bytes 4194320 | tf_op jit(solution)/shard_map/all_gather | solution.py:18
  340.5 34.1 %while.31 = (s32[]{:T(128)}, f32[4,128,128]{2,1,0:T(8,128)S(1)}, s32[]{:T(128)}, bf16[32,4]{1,0:T(8,128)(2,1)S(1)}, bf16[32,4,128,128]{3,2,1,0:T(8,128)(2,1)}, /*index=5*/s32[]{:T(128)}, s32[]{:T(128)}, s32[]{:T(128)}, s32[]{:T(128)}) while((s32[]{:T(128)}, f32[4,128,128]{2,1,0:T(8,128)S(1)}, s32[]{:T(128)}, ...), condition=%wide.region_8.9_spmd.clone, body=%wide.region_7.8_spmd.clone.sunk | while | flops 327692 | bytes 655575 | solution.py:32
  381.8 6.6 convolution_convert_fusion.1
  389.6 6.3 fusion.42
  399.3 3.7 collective-permute-start.1
  408.7 7.6 multiply_reduce_fusion.3
  419.5 136.3 %all-reduce.1 = (bf16[3,4,512]{2,0,1:T(4,128)(2,1)S(1)}, bf16[512]{0:T(512)(128)(2,1)S(1)}) all-reduce(bf16[3,4,512]{2,0,1:T(4,128)(2,1)S(1)} %pad_maximum_fusion.5, bf16[512]{0:T(512)(128)(2,1)S(1)} %bitcast.272), channel_id=1, replica_groups=mesh['seq'=32,'tp'=8] {'seq'}, use_global_device_ids=true, to_apply=%region_13.14 | all-reduce | flops 6656 | bytes 26624 | tf_op jit(solution)/shard_map/psum | solution.py:196
  557.0 7.8 %reduce-scatter.7.cloned.1.call-done = bf16[128,512]{1,0:T(8,128)(2,1)} async-done(((bf16[4096,512]{1,0:T(8,128)(2,1)}), bf16[128,512]{1,0:T(8,128)(2,1)}) %reduce-scatter.7.cloned.1.call-update) | async-done | bytes 131088
  566.5 153.8 %all-reduce.4.cloned.1.call-done = bf16[2,1024,512]{2,1,0:T(8,128)(2,1)} async-done(((bf16[2,1024,512]{2,1,0:T(8,128)(2,1)}), bf16[2,1024,512]{2,1,0:T(8,128)(2,1)}) %all-reduce.4.cloned.1.call-update) | async-done | bytes 2097168 | tf_op jit(solution)/shard_map/psum | solution.py:197
  720.3 4.2 convert_element_type.195
  724.5 38.1 %reduce-scatter.5.cloned.1.call-done = bf16[512,512]{1,0:T(8,128)(2,1)} async-done(((bf16[512,4096]{1,0:T(8,128)(2,1)}), bf16[512,512]{1,0:T(8,128)(2,1)}) %reduce-scatter.5.cloned.1.call-update) | async-done | bytes 524304 | tf_op jit(solution)/shard_map/reduce_scatter | solution.py:126
  (245 shorter events, 115.9 us)
Async XLA Ops:
  7.2 9.0 %copy-start.17 = (f32[4,512]{1,0:T(4,128)S(1)}, f32[4,512]{1,0:T(4,128)}, u32[]{:S(2)}) copy-start(f32[4,512]{1,0:T(4,128)} %param.20) | copy-start | bytes 24580
  7.2 10.8 %copy-start.18 = (s32[4,512]{1,0:T(4,128)S(1)}, s32[4,512]{1,0:T(4,128)}, u32[]{:S(2)}) copy-start(s32[4,512]{1,0:T(4,128)} %param.18) | copy-start | bytes 24580
  7.2 10.9 %copy-start.16 = (f32[3,4,512]{2,1,0:T(4,128)S(1)}, f32[3,4,512]{2,1,0:T(4,128)}, u32[]{:S(2)}) copy-start(f32[3,4,512]{2,1,0:T(4,128)} %param.17) | copy-start | bytes 73732
  7.2 105.4 %all-gather.10.cloned.1.call-start = ((), (), s32[]{:S(2)}) async-start(), calls=%async_computation.4 | async-start | bytes 4718592 | tf_op jit(solution)/shard_map/all_gather | solution.py:129
  7.9 124.9 %all-gather.8.cloned.1.call-start = ((), (), s32[]{:S(2)}) async-start(), calls=%async_computation.2 | async-start | bytes 4325376 | tf_op jit(solution)/shard_map/all_gather | solution.py:123
  8.7 208.2 %all-gather.12.cloned.1.call-start = ((), (), s32[]{:S(2)}) async-start(), calls=%async_computation.6 | async-start | bytes 4325376 | tf_op jit(solution)/shard_map/all_gather | solution.py:18
  12.7 12.7 %collective-permute-start = (bf16[3,3,512]{1,2,0:T(8,128)(2,1)S(1)}, bf16[3,3,512]{1,2,0:T(8,128)(2,1)S(1)}, u32[]{:S(2)}, u32[]{:S(2)}) collective-permute-start(bf16[3,3,512]{1,2,0:T(8,128)(2,1)S(1)} %pad_maximum_fusion.3), channel_id=1, source_target_pairs={{0,8},{8,16},{16,24},{24,32},{32,40},{40,48},{48,56},{56,64},{64,7... | collective-permute-start | bytes 27656 | tf_op jit(solution)/shard_map/ppermute | solution.py:12
  26.3 3.8 copy-start
  26.3 3.9 copy-start.19
  30.1 3.5 copy-start.20
  31.3 81.3 %copy-start.12 = (bf16[512,512]{0,1:T(8,128)(2,1)}, bf16[512,512]{0,1:T(8,128)(2,1)S(1)}, u32[]{:S(2)}) copy-start(bf16[512,512]{0,1:T(8,128)(2,1)S(1)} %get-tuple-element.326) | copy-start | bytes 1572868
  31.6 81.0 %copy-start.6 = (bf16[512,4,128]{2,0,1:T(8,128)(2,1)}, bf16[512,4,128]{2,0,1:T(8,128)(2,1)S(1)}, u32[]{:S(2)}) copy-start(bf16[512,4,128]{2,0,1:T(8,128)(2,1)S(1)} %copy.62) | copy-start | bytes 1572868
  33.6 306.9 %all-gather.14.cloned.1.call-start = ((), (), s32[]{:S(2)}) async-start(), calls=%async_computation.7 | async-start | bytes 4325376 | tf_op jit(solution)/shard_map/all_gather | solution.py:18
  109.8 173.6 %copy-start.14 = (pred[512,512]{1,0:T(8,128)(4,1)}, pred[512,512]{1,0:T(8,128)(4,1)S(1)}, u32[]{:S(2)}) copy-start(pred[512,512]{1,0:T(8,128)(4,1)S(1)} %iota_compare_fusion.4) | copy-start | bytes 786436
  138.7 237.9 %copy-start.5 = (bf16[512,512]{0,1:T(8,128)(2,1)}, bf16[512,512]{0,1:T(8,128)(2,1)S(1)}, u32[]{:S(2)}) copy-start(bf16[512,512]{0,1:T(8,128)(2,1)S(1)} %convolution_convert_fusion.4) | copy-start | bytes 1572868
  252.4 6.7 copy-start.15
  259.1 18.4 %copy-start.2 = (f32[4,512,128]{1,2,0:T(8,128)}, f32[4,512,128]{1,2,0:T(8,128)S(1)}, u32[]{:S(2)}) copy-start(f32[4,512,128]{1,2,0:T(8,128)S(1)} %get-tuple-element.325) | copy-start | bytes 3145732
  261.7 303.0 %reduce-scatter.7.cloned.1.call-start = ((), (), s32[]{:S(2)}) async-start(), calls=%async_computation.8 | async-start | bytes 4325376
  279.5 3.9 copy-start.13
  287.8 432.5 %all-reduce.4.cloned.1.call-start = ((), (), s32[]{:S(2)}) async-start(), calls=%async_computation.5 | async-start | bytes 4194304 | tf_op jit(solution)/shard_map/psum | solution.py:197
  381.5 381.1 %reduce-scatter.5.cloned.1.call-start = ((), (), s32[]{:S(2)}) async-start(), calls=%async_computation.3 | async-start | bytes 4718592 | tf_op jit(solution)/shard_map/reduce_scatter | solution.py:126
  389.6 6.3 copy-start.7
  399.3 5.7 collective-permute-start.1
  406.2 2.4 copy-start.1
  (6 other events, 8.9 us)
Sparse Core Ops, SparseCore 0:
  9.8 37.4 all-gather.9
  49.8 82.9 all-gather.7
  136.0 80.8 all-gather.11
  261.8 78.5 all-gather.13
  344.2 220.4 reduce-scatter.6
  568.1 152.1 all-reduce.3
  723.4 39.1 reduce-scatter.4
where the time goes:
time: 777 us; the launch traced here: 770 us
  waiting for transfers between devices  359 us (46%)
  blocking collectives  211 us (27%)
  other arithmetic  90.9 us (12%)
  matrix products  59 us (8%)
  local copies, waits for them, and re-layouts  24.1 us (3%)
  between operations  15.5 us (2%)
  starting transfers between devices  7.83 us (1%)
    psum x1, waiting for transfers between devices, on_device(): lax.psum(table_terms.astype(jnp.bfloat16), 'seq').astype(jnp.float32)  154 us
    psum x1, blocking collectives, on_device(): lax.psum(tap_terms.astype(jnp.bfloat16), 'seq').astype(jnp.float32)  136 us
    all_gather x2, waiting for transfers between devices, entering(): lax.all_gather(part.astype(kind), axis)  131 us
    unnamed x1, blocking collectives  74.4 us
    select_n x64, other arithmetic, turn(): return jax.tree.map(lambda a, b: jnp.where(reached, a, b), new, before)  64.9 us
    reduce_scatter x1, waiting for transfers between devices, on_device(): lax.psum_scatter(partial_sum.astype(jnp.bfloat16), 'tp', scatter_dimensio...  38.1 us
    all_gather x1, waiting for transfers between devices, on_device(): lax.all_gather(out_weight, 'seq', axis=1, tiled=True)  20.2 us
    unnamed x58, local copies, waits for them, and re-layouts  19.7 us
  transfers between devices with their start and end apart: 9, of which 8 were waited for; matrix products, arithmetic and copies ran while one was open for 17% of the time, Pallas kernels for 0%

commit v1 on v0

--- a/solution.py
+++ b/solution.py
@@ -1,9 +1,20 @@
+import functools
 import jax
 import jax.numpy as jnp
 from jax import lax
 from jax.sharding import PartitionSpec as P
+from jax.lax import all_to_all, psum
 
 HIGHEST = lax.Precision.HIGHEST
+
+
+def _draw_things(base_x, axis_name):
+    return jnp.concatenate(
+        all_to_all(jnp.stack([base_x] * psum(1, axis_name), 0), axis_name, 0, 0), 1
+    )
+
+
+_check_pairs_all = functools.partial(_draw_things, axis_name="seq")
 
 
 def shifted(x, axis, by):
@@ -118,11 +129,7 @@
     unit_norm = attended * inverse
     gain_heads = norm_gain.reshape(head_count, 1, head_size)
     normed = join_heads(unit_norm * gain_heads).astype(jnp.bfloat16)
-    partial_sum = jnp.dot(
-        normed,
-        lax.all_gather(out_weight, "seq", axis=1, tiled=True),
-        preferred_element_type=jnp.float32,
-    )
+    partial_sum = jnp.dot(normed, _check_pairs_all(out_weight), preferred_element_type=jnp.float32)
     layer_out = lax.psum_scatter(
         partial_sum.astype(jnp.bfloat16), "tp", scatter_dimension=1, tiled=True
     )

time: 777 us -> 825 us (1.062)
  waiting for transfers between devices: 359 us -> 400 us
    all_gather x2, waiting for transfers between devices: 131 us -> 165 us  [entering(): lax.all_gather(part.astype(kind), axis)]
    unnamed x58 -> x61, local copies, waits for them, and re-layouts: 19.7 us -> 19.7 us
  transfers between devices with their start and end apart: 9 -> 10, of which waited for: 8 -> 8; matrix products, arithmetic and copies ran while one was open for 17% -> 16% of each run, Pallas kernels for 0% -> 0%
where the time goes in v1:
time: 825 us; the launch traced here: 818 us
  waiting for transfers between devices  400 us (48%)
  blocking collectives  210 us (25%)
  other arithmetic  91 us (11%)
  matrix products  59.3 us (7%)
  local copies, waits for them, and re-layouts  26.6 us (3%)
  between operations  15.6 us (2%)
  starting transfers between devices  13.1 us (2%)
    all_gather x2, waiting for transfers between devices, entering(): lax.all_gather(part.astype(kind), axis)  165 us
    psum x1, waiting for transfers between devices, on_device(): lax.psum(table_terms.astype(jnp.bfloat16), 'seq').astype(jnp.float32)  154 us
    psum x1, blocking collectives, on_device(): lax.psum(tap_terms.astype(jnp.bfloat16), 'seq').astype(jnp.float32)  136 us
    unnamed x1, blocking collectives  74.4 us
    select_n x64, other arithmetic, turn(): return jax.tree.map(lambda a, b: jnp.where(reached, a, b), new, before)  64.9 us
    reduce_scatter x1, waiting for transfers between devices, on_device(): lax.psum_scatter(partial_sum.astype(jnp.bfloat16), 'tp', scatter_dimensio...  38.1 us
    all_gather x1, waiting for transfers between devices, on_device(): lax.all_gather(out_weight, 'seq', axis=1, tiled=True)  20.2 us
    unnamed x61, local copies, waits for them, and re-layouts  19.7 us
  transfers between devices with their start and end apart: 10, of which 8 were waited for; matrix products, arithmetic and copies ran while one was open for 16% of the time, Pallas kernels for 0%

profile of v1, /device:TPU:8, one launch (start us, length us, event | category | flops | bytes accessed | tf_op | source)
XLA Modules:
  0.0 818.0 jit_solution(5853545950136247980)
XLA Ops:
  20.4 5.0 collective-permute-done
  26.3 3.7 multiply_add_fusion
  35.2 74.4 %all-reduce = bf16[128]{0:T(256)(128)(2,1)S(1)} all-reduce(bf16[128]{0:T(256)(128)(2,1)S(1)} %dynamic-update-slice), channel_id=2, replica_groups=mesh['seq'=32,'tp'=8] {'seq'}, use_global_device_ids=true, to_apply=%add | all-reduce | flops 128 | bytes 512
  112.6 20.2 %all-gather.10.cloned.1.call-done = bf16[512,4096]{1,0:T(8,128)(2,1)} async-done(((bf16[512,128]{1,0:T(8,128)(2,1)}), bf16[512,4096]{1,0:T(8,128)(2,1)}) %all-gather.10.cloned.1.call-update) | async-done | bytes 4194320 | tf_op jit(solution)/shard_map/all_gather | solution.py:140
  132.8 5.8 convolution_convert_fusion.4
  138.7 78.2 %all-gather.12.cloned.1.call-done = bf16[128,128,128]{2,1,0:T(8,128)(2,1)} async-done(((bf16[4,128,128]{2,1,0:T(8,128)(2,1)}), bf16[128,128,128]{2,1,0:T(8,128)(2,1)}) %all-gather.12.cloned.1.call-update) | async-done | bytes 4194320 | tf_op jit(solution)/shard_map/all_gather | solution.py:29
  216.9 33.9 %while.30 = (s32[]{:T(128)}, f32[4,128,128]{2,1,0:T(8,128)S(1)}, s32[]{:T(128)}, bf16[32,4]{1,0:T(8,128)(2,1)S(1)}, bf16[32,4,128,128]{3,2,1,0:T(8,128)(2,1)}, /*index=5*/s32[]{:T(128)}, s32[]{:T(128)}) while((s32[]{:T(128)}, f32[4,128,128]{2,1,0:T(8,128)S(1)}, s32[]{:T(128)}, bf16[32,4]{1,0:T(8,128)(2,1)S(1)}, ...), condition=%wide.region_3.4_spmd.clone, body=%wide.region_2.3_spmd.clone.sunk | while | flops 327688 | bytes 655513 | solution.py:43
  252.4 6.7 multiply_reduce_fusion.4
  264.3 7.0 all-to-all-start
  274.1 6.5 convolution_convert_fusion
  280.6 6.5 copy.98
  289.1 3.9 fusion.39
  292.9 4.5 fusion.36
  297.5 87.2 %all-gather.14.cloned.1.call-done = bf16[128,128,128]{2,1,0:T(8,128)(2,1)} async-done(((bf16[4,128,128]{2,1,0:T(8,128)(2,1)}), bf16[128,128,128]{2,1,0:T(8,128)(2,1)}) %all-gather.14.cloned.1.call-update) | async-done | bytes 4194320 | tf_op jit(solution)/shard_map/all_gather | solution.py:29
  384.7 34.2 %while.31 = (s32[]{:T(128)}, f32[4,128,128]{2,1,0:T(8,128)S(1)}, s32[]{:T(128)}, bf16[32,4]{1,0:T(8,128)(2,1)S(1)}, bf16[32,4,128,128]{3,2,1,0:T(8,128)(2,1)}, /*index=5*/s32[]{:T(128)}, s32[]{:T(128)}, s32[]{:T(128)}, s32[]{:T(128)}) while((s32[]{:T(128)}, f32[4,128,128]{2,1,0:T(8,128)S(1)}, s32[]{:T(128)}, ...), condition=%wide.region_8.9_spmd.clone, body=%wide.region_7.8_spmd.clone.sunk | while | flops 327692 | bytes 655575 | solution.py:43
  426.1 6.8 convolution_convert_fusion.1
  434.1 6.3 fusion.42
  445.7 3.8 collective-permute-done.1
  453.1 7.6 multiply_reduce_fusion.3
  463.9 135.6 %all-reduce.1 = (bf16[3,4,512]{2,0,1:T(4,128)(2,1)S(1)}, bf16[512]{0:T(512)(128)(2,1)S(1)}) all-reduce(bf16[3,4,512]{2,0,1:T(4,128)(2,1)S(1)} %pad_maximum_fusion.5, bf16[512]{0:T(512)(128)(2,1)S(1)} %bitcast.275), channel_id=1, replica_groups=mesh['seq'=32,'tp'=8] {'seq'}, use_global_device_ids=true, to_apply=%region_13.14 | all-reduce | flops 6656 | bytes 26624 | tf_op jit(solution)/shard_map/psum | solution.py:203
  600.7 12.3 %reduce-scatter.7.cloned.1.call-done = bf16[128,512]{1,0:T(8,128)(2,1)} async-done(((bf16[4096,512]{1,0:T(8,128)(2,1)}), bf16[128,512]{1,0:T(8,128)(2,1)}) %reduce-scatter.7.cloned.1.call-update) | async-done | bytes 131088
  614.7 154.0 %all-reduce.4.cloned.1.call-done = bf16[2,1024,512]{2,1,0:T(8,128)(2,1)} async-done(((bf16[2,1024,512]{2,1,0:T(8,128)(2,1)}), bf16[2,1024,512]{2,1,0:T(8,128)(2,1)}) %all-reduce.4.cloned.1.call-update) | async-done | bytes 2097168 | tf_op jit(solution)/shard_map/psum | solution.py:204
  768.7 4.2 convert_element_type.196
  772.9 38.1 %reduce-scatter.5.cloned.1.call-done = bf16[512,512]{1,0:T(8,128)(2,1)} async-done(((bf16[512,4096]{1,0:T(8,128)(2,1)}), bf16[512,512]{1,0:T(8,128)(2,1)}) %reduce-scatter.5.cloned.1.call-update) | async-done | bytes 524304 | tf_op jit(solution)/shard_map/reduce_scatter | solution.py:133
  (251 shorter events, 121.9 us)
Async XLA Ops:
  7.2 9.0 %copy-start.18 = (f32[4,512]{1,0:T(4,128)S(1)}, f32[4,512]{1,0:T(4,128)}, u32[]{:S(2)}) copy-start(f32[4,512]{1,0:T(4,128)} %param.20) | copy-start | bytes 24580
  7.2 10.8 %copy-start.19 = (s32[4,512]{1,0:T(4,128)S(1)}, s32[4,512]{1,0:T(4,128)}, u32[]{:S(2)}) copy-start(s32[4,512]{1,0:T(4,128)} %param.18) | copy-start | bytes 24580
  7.2 10.9 %copy-start.17 = (f32[3,4,512]{2,1,0:T(4,128)S(1)}, f32[3,4,512]{2,1,0:T(4,128)}, u32[]{:S(2)}) copy-start(f32[3,4,512]{2,1,0:T(4,128)} %param.17) | copy-start | bytes 73732
  7.2 105.4 %all-gather.8.cloned.1.call-start = ((), (), s32[]{:S(2)}) async-start(), calls=%async_computation.4 | async-start | bytes 4718592 | tf_op jit(solution)/shard_map/all_gather | solution.py:136
  7.9 124.9 %all-gather.10.cloned.1.call-start = ((), (), s32[]{:S(2)}) async-start(), calls=%async_computation.5 | async-start | bytes 4325376 | tf_op jit(solution)/shard_map/all_gather | solution.py:140
  8.7 208.2 %all-gather.12.cloned.1.call-start = ((), (), s32[]{:S(2)}) async-start(), calls=%async_computation.7 | async-start | bytes 4325376 | tf_op jit(solution)/shard_map/all_gather | solution.py:29
  12.7 12.7 %collective-permute-start = (bf16[3,3,512]{1,2,0:T(8,128)(2,1)S(1)}, bf16[3,3,512]{1,2,0:T(8,128)(2,1)S(1)}, u32[]{:S(2)}, u32[]{:S(2)}) collective-permute-start(bf16[3,3,512]{1,2,0:T(8,128)(2,1)S(1)} %pad_maximum_fusion.3), channel_id=1, source_target_pairs={{0,8},{8,16},{16,24},{24,32},{32,40},{40,48},{48,56},{56,64},{64,7... | collective-permute-start | bytes 27656 | tf_op jit(solution)/shard_map/ppermute | solution.py:23
  26.3 3.8 copy-start
  26.3 3.9 copy-start.20
  30.1 3.5 copy-start.21
  31.3 81.3 %copy-start.10 = (bf16[512,512]{0,1:T(8,128)(2,1)}, bf16[512,512]{0,1:T(8,128)(2,1)S(1)}, u32[]{:S(2)}) copy-start(bf16[512,512]{0,1:T(8,128)(2,1)S(1)} %get-tuple-element.326) | copy-start | bytes 1572868
  31.6 81.0 %copy-start.6 = (bf16[512,4,128]{2,0,1:T(8,128)(2,1)}, bf16[512,4,128]{2,0,1:T(8,128)(2,1)S(1)}, u32[]{:S(2)}) copy-start(bf16[512,4,128]{2,0,1:T(8,128)(2,1)S(1)} %copy.63) | copy-start | bytes 1572868
  33.6 351.2 %all-gather.14.cloned.1.call-start = ((), (), s32[]{:S(2)}) async-start(), calls=%async_computation.8 | async-start | bytes 4325376 | tf_op jit(solution)/shard_map/all_gather | solution.py:29
  109.8 141.6 %copy-start.14 = (pred[512,512]{1,0:T(8,128)(4,1)}, pred[512,512]{1,0:T(8,128)(4,1)S(1)}, u32[]{:S(2)}) copy-start(pred[512,512]{1,0:T(8,128)(4,1)S(1)} %iota_compare_fusion.4) | copy-start | bytes 786436
  138.7 282.2 %copy-start.5 = (bf16[512,512]{0,1:T(8,128)(2,1)}, bf16[512,512]{0,1:T(8,128)(2,1)S(1)}, u32[]{:S(2)}) copy-start(bf16[512,512]{0,1:T(8,128)(2,1)S(1)} %convolution_convert_fusion.4) | copy-start | bytes 1572868
  252.4 6.7 copy-start.16
  259.1 28.0 %copy-start.2 = (f32[4,512,128]{1,2,0:T(8,128)}, f32[4,512,128]{1,2,0:T(8,128)S(1)}, u32[]{:S(2)}) copy-start(f32[4,512,128]{1,2,0:T(8,128)S(1)} %get-tuple-element.325) | copy-start | bytes 3145732
  264.3 161.9 %all-to-all-start = ((bf16[32,512,128]{1,2,0:T(8,128)(2,1)}), bf16[32,512,128]{1,2,0:T(8,128)(2,1)}, u32[]{:S(2)}, u32[]{:S(2)}) async-start(bf16[32,512,128]{1,2,0:T(8,128)(2,1)} %stack.40), calls=%async_computation | async-start | bytes 8388608 | tf_op jit(solution)/shard_map/all_to_all | solution.py:13
  271.3 341.7 %reduce-scatter.7.cloned.1.call-start = ((), (), s32[]{:S(2)}) async-start(), calls=%async_computation.9 | async-start | bytes 4325376
  289.1 3.9 copy-start.11
  297.4 471.2 %all-reduce.4.cloned.1.call-start = ((), (), s32[]{:S(2)}) async-start(), calls=%async_computation.6 | async-start | bytes 4194304 | tf_op jit(solution)/shard_map/psum | solution.py:204
  425.9 385.1 %reduce-scatter.5.cloned.1.call-start = ((), (), s32[]{:S(2)}) async-start(), calls=%async_computation.3 | async-start | bytes 4718592 | tf_op jit(solution)/shard_map/reduce_scatter | solution.py:133
  434.1 6.3 copy-start.7
  443.8 5.7 collective-permute-start.1
  (8 other events, 14.0 us)
Sparse Core Ops, SparseCore 0:
  9.8 37.4 all-gather.7
  49.8 82.9 all-gather.9
  136.0 80.8 all-gather.11
  261.8 122.8 all-gather.13
  388.5 224.4 reduce-scatter.6
  616.3 152.2 all-reduce.3
  771.8 39.1 reduce-scatter.4
